TPU v7x, 32 devices: a whole 2x2x4 slice. The times are simulated.
32 devices in a mesh: samp: 8 (over z, y), feat: 4 (over x, core).
Axes of the slice: x: 2, y: 2, z: 4, core: 2. Of those that a mesh axis runs over, the one named last changes fastest.
Arguments:
- layer_input: bfloat16 [512, 64, 512], P('samp', 'feat'), may hold values from -6 to 6
- segment_ids: int32 [512], replicated, may hold values from 0 to 3, as said below
- context_flags: int32 [512], replicated, may hold values from 0 to 1, as said below
- first_gain: float32 [512], replicated, may hold values from 0.1 to 1.9
- first_shift: float32 [512], replicated, may hold values from -3 to 3
- sample_weight: bfloat16 [512, 1536], replicated, may hold values from -0.25 to 0.25
- sample_bias: float32 [1024], replicated, may hold values from -3 to 3
- sample_mixer: bfloat16 [512, 512], replicated, may hold values from -1 to 1
- sample_offset: float32 [512], replicated, may hold values from -3 to 3
- second_gain: float32 [512], replicated, may hold values from 0.1 to 1.9
- second_shift: float32 [512], replicated, may hold values from -3 to 3
- feature_weight: bfloat16 [512, 1536], replicated, may hold values from -0.25 to 0.25
- feature_bias: float32 [1024], replicated, may hold values from -3 to 3
- feature_mixer: bfloat16 [512, 512], replicated, may hold values from -1.5 to 1.5
- feature_offset: float32 [512], replicated, may hold values from -3 to 3
- third_gain: float32 [512], replicated, may hold values from 0.1 to 1.9
- third_shift: float32 [512], replicated, may hold values from -3 to 3
- expand_weight: bfloat16 [512, 2048], replicated, may hold values from -0.25 to 0.25
- expand_bias: float32 [2048], replicated, may hold values from -3 to 3
- reduce_weight: bfloat16 [2048, 512], replicated, may hold values from -0.125 to 0.125
- reduce_bias: float32 [512], replicated, may hold values from -3 to 3
- cotangent: bfloat16 [512, 64, 512], P('samp', 'feat'), may hold values from -6 to 6
Outputs:
- layer_output: bfloat16 [512, 64, 512], P('samp', 'feat')
- input_grad: bfloat16 [512, 64, 512], P('samp', 'feat')
- first_gain_grad: float32 [512], P('samp')
- first_shift_grad: float32 [512], P('samp')
- sample_weight_grad: float32 [512, 1536], P('samp')
- sample_bias_grad: float32 [1024], P('samp')
- sample_mixer_grad: float32 [512, 512], P('samp')
- sample_offset_grad: float32 [512], P('samp')
- second_gain_grad: float32 [512], P('samp')
- second_shift_grad: float32 [512], P('samp')
- feature_weight_grad: float32 [512, 1536], P('samp')
- feature_bias_grad: float32 [1024], P('samp')
- feature_mixer_grad: float32 [512, 512], P('samp')
- feature_offset_grad: float32 [512], P('samp')
- third_gain_grad: float32 [512], P('samp')
- third_shift_grad: float32 [512], P('samp')
- expand_weight_grad: float32 [512, 2048], P('samp')
- expand_bias_grad: float32 [2048], P('samp')
- reduce_weight_grad: float32 [2048, 512], P('samp')
- reduce_bias_grad: float32 [512], P('samp')
Inputs may be any that keep to these rules, and one draw needn't show every extreme that they name: `context_flags`: the samples of one index of samp (an aligned block of 64 samples) are all context samples or all query samples; exactly 1 block are context blocks, which ones is drawn. `segment_ids`: every task holds exactly 16 context samples.
All inputs are finite; a program needn't handle non-finite values.
Results may differ from a plain program's by a relative error of at most 0.017.
Values may be sent and summed in bfloat16 or wider, within the bound.
No kernel may reach another device: no remote copies, remote signals or barrier semaphores. Data moves between devices by JAX's collectives and lax.ppermute only.
A program may use at most 256 MiB of HBM per device.

v0:
```python
from functools import partial
import jax
import jax.numpy as jnp
from jax import lax
from jax.sharding import PartitionSpec as P

HEADS = 8
HEAD_DIM = 64
EPS = 1e-05
MASKED = -1000000000.0


def spread_2(block, axis, owner):
    block = jnp.where(lax.axis_index(axis) == owner, block, jnp.zeros_like(block))
    return lax.psum(block, axis)


def layer_norm(values, gain_row, shift_row):
    center = jnp.mean(values, axis=-1, keepdims=True)
    spread = values - center
    variance = jnp.mean(spread * spread, axis=-1, keepdims=True)
    return spread * lax.rsqrt(variance + EPS) * gain_row + shift_row


def apply_weight(active, weight):
    return jnp.einsum("sfd,de->sfe", active, weight, preferred_element_type=jnp.float32)


def input_back(grad_out, weight):
    return jnp.einsum("sfe,de->sfd", grad_out, weight, preferred_element_type=jnp.float32)


def weight_grad(active, grad_out):
    return jnp.einsum("sfd,sfe->de", active, grad_out, preferred_element_type=jnp.float32)


def column_sum(values):
    return jnp.sum(values.astype(jnp.float32), axis=(0, 1))


def project(active, weight, bias_row):
    model_width = active.shape[-1]
    joined = apply_weight(active, weight)
    queries = (joined[..., :model_width] + bias_row[:model_width]).astype(jnp.bfloat16)
    key_part = joined[..., model_width : 2 * model_width].astype(jnp.bfloat16)
    value_part = (joined[..., 2 * model_width :] + bias_row[model_width:]).astype(jnp.bfloat16)
    return (queries, key_part, value_part)


def split_heads(values):
    return values.reshape(values.shape[0], values.shape[1], HEADS, HEAD_DIM)


def join_heads(values):
    return values.reshape(values.shape[0], values.shape[1], HEADS * HEAD_DIM)


def soft_weights(scores):
    top_score = jnp.max(scores, axis=-1, keepdims=True)
    raised = jnp.exp(scores - top_score)
    return raised / jnp.sum(raised, axis=-1, keepdims=True)


def feature_attend(queries, key_part, value_part):
    score_scale = HEAD_DIM ** (-0.5)
    scores = (
        jnp.einsum(
            "sfhd,sghd->shfg",
            split_heads(queries),
            split_heads(key_part),
            preferred_element_type=jnp.float32,
        )
        * score_scale
    )
    probability = soft_weights(scores)
    mixed = jnp.einsum(
        "shfg,sghd->sfhd",
        probability.astype(jnp.bfloat16),
        split_heads(value_part),
        preferred_element_type=jnp.float32,
    )
    return (join_heads(mixed).astype(jnp.bfloat16), probability)


def feature_grads(queries, key_part, value_part, probability, grad_mixed):
    score_scale = HEAD_DIM ** (-0.5)
    grad_heads = split_heads(grad_mixed)
    grad_weights = jnp.einsum(
        "sfhd,sghd->shfg", grad_heads, split_heads(value_part), preferred_element_type=jnp.float32
    )
    inner_sum = jnp.sum(probability * grad_weights, axis=-1, keepdims=True)
    grad_scores = (probability * (grad_weights - inner_sum)).astype(jnp.bfloat16)
    grad_queries = (
        jnp.einsum(
            "shfg,sghd->sfhd",
            grad_scores,
            split_heads(key_part),
            preferred_element_type=jnp.float32,
        )
        * score_scale
    )
    grad_keys = (
        jnp.einsum(
            "shfg,sfhd->sghd", grad_scores, split_heads(queries), preferred_element_type=jnp.float32
        )
        * score_scale
    )
    grad_values = jnp.einsum(
        "shfg,sfhd->sghd",
        probability.astype(jnp.bfloat16),
        grad_heads,
        preferred_element_type=jnp.float32,
    )
    return (join_heads(grad_queries), join_heads(grad_keys), join_heads(grad_values))


def local(
    layer_input,
    segment_ids,
    context_flags,
    first_gain,
    first_shift,
    sample_weight,
    sample_bias,
    sample_mixer,
    sample_offset,
    second_gain,
    second_shift,
    feature_weight,
    feature_bias,
    feature_mixer,
    feature_offset,
    third_gain,
    third_shift,
    expand_weight,
    expand_bias,
    reduce_weight,
    reduce_bias,
    cotangent,
):
    sample_rows = layer_input.shape[0]
    feature_rows = layer_input.shape[1]
    model_width = layer_input.shape[2]
    score_scale = HEAD_DIM ** (-0.5)
    shard_count = lax.axis_size("samp")
    context_shards = shard_count // 8
    total_context = context_shards * sample_rows
    residual_zero = layer_input.astype(jnp.float32)
    normed_one, norm_one_back = jax.vjp(layer_norm, residual_zero, first_gain, first_shift)
    active_one = normed_one.astype(jnp.bfloat16)
    queries_one, keys_one, values_one = project(active_one, sample_weight, sample_bias)
    my_index = lax.axis_index("samp")
    shard_flags = context_flags.reshape(shard_count, sample_rows)[:, 0]
    shard_rank = jnp.cumsum(shard_flags) - 1
    shard_ids = jnp.arange(shard_count, dtype=jnp.int32)
    slot_ids = jnp.arange(context_shards, dtype=jnp.int32)
    root_hits = (shard_rank[None, :] == slot_ids[:, None]) & (shard_flags[None, :] == 1)
    roots = jnp.sum(jnp.where(root_hits, shard_ids[None, :], 0), axis=1)
    context_tasks = jnp.take(segment_ids.reshape(shard_count, sample_rows), roots, axis=0).reshape(
        total_context
    )
    local_tasks = lax.dynamic_slice_in_dim(segment_ids, my_index * sample_rows, sample_rows)
    allowed = local_tasks[:, None] == context_tasks[None, :]
    is_context = shard_flags[my_index] == 1
    own_rank = jnp.maximum(shard_rank[my_index], 0)
    own_block = jnp.concatenate([keys_one, values_one], axis=-1)

    def fetch_rows(step, buffer):
        piece = spread_2(own_block, "samp", roots[step])
        return lax.dynamic_update_slice_in_dim(buffer, piece, step * sample_rows, 0)

    empty_rows = jnp.zeros((total_context, feature_rows, 2 * model_width), jnp.bfloat16)
    fetched = lax.fori_loop(0, context_shards, fetch_rows, empty_rows)
    context_keys = fetched[..., :model_width]
    context_values = fetched[..., model_width:]
    query_heads = split_heads(queries_one)
    key_heads = split_heads(context_keys)
    value_heads = split_heads(context_values)
    scores = (
        jnp.einsum("sfhd,cfhd->fhsc", query_heads, key_heads, preferred_element_type=jnp.float32)
        * score_scale
    )
    sample_prob = soft_weights(jnp.where(allowed[None, None], scores, MASKED))
    sample_weights = sample_prob.astype(jnp.bfloat16)
    mixed_one = join_heads(
        jnp.einsum(
            "fhsc,cfhd->sfhd", sample_weights, value_heads, preferred_element_type=jnp.float32
        )
    ).astype(jnp.bfloat16)
    residual_one = residual_zero + apply_weight(mixed_one, sample_mixer) + sample_offset
    normed_two, norm_two_back = jax.vjp(layer_norm, residual_one, second_gain, second_shift)
    active_two = normed_two.astype(jnp.bfloat16)
    queries_two, keys_two, values_two = project(active_two, feature_weight, feature_bias)
    all_keys, all_values = (
        lax.all_gather(keys_two, "feat", axis=1, tiled=True),
        lax.all_gather(values_two, "feat", axis=1, tiled=True),
    )
    mixed_two, feature_prob = feature_attend(queries_two, all_keys, all_values)
    residual_two = residual_one + apply_weight(mixed_two, feature_mixer) + feature_offset
    normed_three, norm_three_back = jax.vjp(layer_norm, residual_two, third_gain, third_shift)
    active_three = normed_three.astype(jnp.bfloat16)
    expanded = apply_weight(active_three, expand_weight) + expand_bias
    activated, gelu_back = jax.vjp(partial(jax.nn.gelu, approximate=False), expanded)
    hidden = activated.astype(jnp.bfloat16)
    layer_output = (residual_two + apply_weight(hidden, reduce_weight) + reduce_bias).astype(
        jnp.bfloat16
    )
    grad_out = cotangent.astype(jnp.float32)
    grad_branch = cotangent
    reduce_bias_grad = column_sum(grad_branch)
    reduce_weight_grad = weight_grad(hidden, grad_branch)
    grad_hidden = input_back(grad_branch, reduce_weight).astype(jnp.bfloat16)
    grad_expanded = gelu_back(grad_hidden.astype(jnp.float32))[0].astype(jnp.bfloat16)
    expand_bias_grad = column_sum(grad_expanded)
    expand_weight_grad = weight_grad(active_three, grad_expanded)
    grad_norm, third_gain_grad, third_shift_grad = norm_three_back(
        input_back(grad_expanded, expand_weight)
    )
    grad_two = grad_out + grad_norm
    grad_branch = grad_two.astype(jnp.bfloat16)
    feature_offset_grad = column_sum(grad_branch)
    feature_mixer_grad = weight_grad(mixed_two, grad_branch)
    grad_mixed = input_back(grad_branch, feature_mixer).astype(jnp.bfloat16)
    grad_queries, grad_keys, grad_values = feature_grads(
        queries_two, all_keys, all_values, feature_prob, grad_mixed
    )
    own_key_grads, own_value_grads = (
        lax.psum_scatter(grad_keys, "feat", scatter_dimension=1, tiled=True),
        lax.psum_scatter(grad_values, "feat", scatter_dimension=1, tiled=True),
    )
    grad_project = jnp.concatenate(
        [
            grad_queries.astype(jnp.bfloat16),
            own_key_grads.astype(jnp.bfloat16),
            own_value_grads.astype(jnp.bfloat16),
        ],
        axis=-1,
    )
    feature_weight_grad = weight_grad(active_two, grad_project)
    feature_bias_grad = jnp.concatenate(
        [
            column_sum(grad_project[..., :model_width]),
            column_sum(grad_project[..., 2 * model_width :]),
        ]
    )
    grad_norm, second_gain_grad, second_shift_grad = norm_two_back(
        input_back(grad_project, feature_weight)
    )
    grad_one = grad_two + grad_norm
    grad_branch = grad_one.astype(jnp.bfloat16)
    sample_offset_grad = column_sum(grad_branch)
    sample_mixer_grad = weight_grad(mixed_one, grad_branch)
    grad_heads = split_heads(input_back(grad_branch, sample_mixer).astype(jnp.bfloat16))
    grad_weights = jnp.einsum(
        "sfhd,cfhd->fhsc", grad_heads, value_heads, preferred_element_type=jnp.float32
    )
    inner_sum = jnp.sum(sample_prob * grad_weights, axis=-1, keepdims=True)
    grad_scores = (sample_prob * (grad_weights - inner_sum)).astype(jnp.bfloat16)
    grad_queries = (
        join_heads(
            jnp.einsum(
                "fhsc,cfhd->sfhd", grad_scores, key_heads, preferred_element_type=jnp.float32
            )
        )
        * score_scale
    ).astype(jnp.bfloat16)
    key_terms = (
        join_heads(
            jnp.einsum(
                "fhsc,sfhd->cfhd", grad_scores, query_heads, preferred_element_type=jnp.float32
            )
        )
        * score_scale
    )
    value_terms = join_heads(
        jnp.einsum(
            "fhsc,sfhd->cfhd", sample_weights, grad_heads, preferred_element_type=jnp.float32
        )
    )
    term_block = jnp.concatenate([key_terms, value_terms], axis=-1)
    summed_terms = lax.psum_scatter(term_block, "samp", scatter_dimension=0, tiled=True)
    summed_rows = lax.all_gather(summed_terms.astype(jnp.bfloat16), "samp", axis=0, tiled=True)
    own_grads = lax.dynamic_slice_in_dim(summed_rows, own_rank * sample_rows, sample_rows, 0)
    own_grads = jnp.where(is_context, own_grads, jnp.zeros_like(own_grads))
    grad_project = jnp.concatenate([grad_queries, own_grads], axis=-1)
    sample_weight_grad = weight_grad(active_one, grad_project)
    sample_bias_grad = jnp.concatenate(
        [column_sum(grad_queries), column_sum(own_grads[..., model_width:])]
    )
    grad_norm, first_gain_grad, first_shift_grad = norm_one_back(
        input_back(grad_project, sample_weight)
    )
    input_grad = (grad_one + grad_norm).astype(jnp.bfloat16)
    summed = lax.psum(
        (
            first_gain_grad,
            first_shift_grad,
            sample_weight_grad,
            sample_bias_grad,
            sample_mixer_grad,
            sample_offset_grad,
            second_gain_grad,
            second_shift_grad,
            feature_weight_grad,
            feature_bias_grad,
            feature_mixer_grad,
            feature_offset_grad,
            third_gain_grad,
            third_shift_grad,
            expand_weight_grad,
            expand_bias_grad,
            reduce_weight_grad,
            reduce_bias_grad,
        ),
        "feat",
    )
    shares = (
        lax.psum_scatter(summed[0], "samp", scatter_dimension=0, tiled=True),
        lax.psum_scatter(summed[1], "samp", scatter_dimension=0, tiled=True),
        lax.psum_scatter(summed[2], "samp", scatter_dimension=0, tiled=True),
        lax.psum_scatter(summed[3], "samp", scatter_dimension=0, tiled=True),
        lax.psum_scatter(summed[4], "samp", scatter_dimension=0, tiled=True),
        lax.psum_scatter(summed[5], "samp", scatter_dimension=0, tiled=True),
        lax.psum_scatter(summed[6], "samp", scatter_dimension=0, tiled=True),
        lax.psum_scatter(summed[7], "samp", scatter_dimension=0, tiled=True),
        lax.psum_scatter(summed[8], "samp", scatter_dimension=0, tiled=True),
        lax.psum_scatter(summed[9], "samp", scatter_dimension=0, tiled=True),
        lax.psum_scatter(summed[10], "samp", scatter_dimension=0, tiled=True),
        lax.psum_scatter(summed[11], "samp", scatter_dimension=0, tiled=True),
        lax.psum_scatter(summed[12], "samp", scatter_dimension=0, tiled=True),
        lax.psum_scatter(summed[13], "samp", scatter_dimension=0, tiled=True),
        lax.psum_scatter(summed[14], "samp", scatter_dimension=0, tiled=True),
        lax.psum_scatter(summed[15], "samp", scatter_dimension=0, tiled=True),
        lax.psum_scatter(summed[16], "samp", scatter_dimension=0, tiled=True),
        lax.psum_scatter(summed[17], "samp", scatter_dimension=0, tiled=True),
    )
    return (
        layer_output,
        input_grad,
        shares[0],
        shares[1],
        shares[2],
        shares[3],
        shares[4],
        shares[5],
        shares[6],
        shares[7],
        shares[8],
        shares[9],
        shares[10],
        shares[11],
        shares[12],
        shares[13],
        shares[14],
        shares[15],
        shares[16],
        shares[17],
    )


def solution(mesh):
    return jax.shard_map(
        local,
        mesh=mesh,
        in_specs=(
            P("samp", "feat", None),
            P(),
            P(),
            P(),
            P(),
            P(),
            P(),
            P(),
            P(),
            P(),
            P(),
            P(),
            P(),
            P(),
            P(),
            P(),
            P(),
            P(),
            P(),
            P(),
            P(),
            P("samp", "feat", None),
        ),
        out_specs=(
            P("samp", "feat", None),
            P("samp", "feat", None),
            P("samp"),
            P("samp"),
            P("samp", None),
            P("samp"),
            P("samp", None),
            P("samp"),
            P("samp"),
            P("samp"),
            P("samp", None),
            P("samp"),
            P("samp", None),
            P("samp"),
            P("samp"),
            P("samp"),
            P("samp", None),
            P("samp"),
            P("samp", None),
            P("samp"),
        ),
        check_vma=False,
    )
```

profile of v0, /device:TPU:0, one launch (start us, length us, event | category | flops | bytes accessed | tf_op | source)
XLA Modules:
  0.0 1231.0 jit_solution(3453029801898814704)
XLA Ops:
  22.2 3.9 fusion.41
  33.9 98.7 %all-reduce.18.cloned.1.call-done = bf16[64,16,1024]{2,1,0:T(8,128)(2,1)} async-done(((bf16[64,16,1024]{2,1,0:T(8,128)(2,1)}), bf16[64,16,1024]{2,1,0:T(8,128)(2,1)}) %all-reduce.18.cloned.1.call-update) | async-done | bytes 2097168 | tf_op jit(solution)/shard_map/while/body/eval_jaxpr/psum | solution.py:15
  135.7 3.9 reshape.296
  139.6 3.9 reshape.293
  143.4 4.0 fusion.68
  165.5 3.9 fusion.40
  171.8 28.0 %all-gather.6.cloned.1.call-done = bf16[64,64,512]{2,1,0:T(8,128)(2,1)} async-done(((bf16[64,16,512]{2,1,0:T(8,128)(2,1)}), bf16[64,64,512]{2,1,0:T(8,128)(2,1)}) %all-gather.6.cloned.1.call-update) | async-done | bytes 4194320 | tf_op jit(solution)/shard_map/all_gather | solution.py:195
  199.8 11.4 reshape.299
  211.1 8.5 fusion.21
  224.9 11.6 all-gather.4.cloned.1.call-done
  236.5 11.2 reshape.297
  247.6 19.4 %convert_bitcast_fusion = bf16[64,16,8,64]{3,1,2,0:T(8,128)(2,1)} fusion(bf16[64,64,8,64]{3,2,1,0:T(8,128)(2,1)} %reshape.297, f32[64,8,16]{2,1,0:T(8,128)S(1)} %get-tuple-element.115, f32[64,8,16,64]{3,2,1,0:T(8,128)} %copy-done.10), kind=kOutput, calls=%fused_computation.111 | convolution fusion | flops 70262848 | bytes 7372800 | tf_op jit(solution)/shard_map/shfg,sghd->sfhd/dot_general | solution.py:76
  277.5 21.9 %multiply_convert_fusion = (bf16[64,16,2048]{2,1,0:T(8,128)(2,1)}, f32[64,16,2048]{2,1,0:T(8,128)S(1)}, f32[64,16,2048]{2,1,0:T(8,128)}) fusion(f32[2048]{0:T(1024)S(1)} %copy-done.73, bf16[512,2048]{1,0:T(8,128)(2,1)S(1)} %copy-done, f32[64,16,512]{2,1,0:T(8,128)S(1)} %get-tuple-element.118, f32[512]{0:T(512)S(1)} %copy-done.75, f32[512]{0:T(512)S(1)} %copy-done.65, ...), kind=kOutput, calls=%fused_computation.15 | convolution fusion | flops 2288517120 | bytes 25186304 | tf_op jit(solution)/shard_map/sfd,de->sfe/dot_general | solution.py:26
  299.4 7.9 convert_reduce_fusion
  318.5 23.3 %fusion.62 = f32[64,8,64,64]{3,2,1,0:T(8,128)} fusion(bf16[64,16,8,64]{3,2,1,0:T(8,128)(2,1)S(1)} %reshape.300, f32[64,8,16]{2,1,0:T(8,128)S(1)} %get-tuple-element.115, f32[64,8,16,64]{3,2,1,0:T(8,128)} %copy-done.10), kind=kOutput, calls=%fused_computation.126 | convolution fusion | flops 69738560 | bytes 11567104 | tf_op jit(solution)/shard_map/shfg,sfhd->sghd/dot_general | solution.py:108
  341.8 12.7 %copy.199 = f32[64,64,512]{2,1,0:T(8,128)} copy(f32[64,64,512]{1,2,0:T(8,128)} %bitcast.119) | data formatting | bytes 16777216 | tf_op jit(solution)/shard_map/reshape | solution.py:55
  354.6 9.1 multiply_reduce_fusion.1
  366.2 7.4 convolution_multiply_fusion
  373.6 12.9 %copy.197 = f32[64,64,512]{2,1,0:T(8,128)} copy(f32[64,64,512]{1,2,0:T(8,128)} %bitcast.116) | data formatting | bytes 16777216 | tf_op jit(solution)/shard_map/reshape | solution.py:55
  388.3 6.3 convert_reduce_fusion.1
  397.4 29.0 %reduce-scatter.12.cloned.1.call-done = f32[64,16,512]{2,1,0:T(8,128)} async-done(((f32[64,64,512]{2,1,0:T(8,128)}), f32[64,16,512]{2,1,0:T(8,128)}) %reduce-scatter.12.cloned.1.call-update) | async-done | bytes 2097168 | tf_op jit(solution)/shard_map/reduce_scatter | solution.py:229
  429.8 71.0 %reduce-scatter.10.cloned.1.call-done = f32[64,16,512]{2,1,0:T(8,128)} async-done(((f32[64,64,512]{2,1,0:T(8,128)}), f32[64,16,512]{2,1,0:T(8,128)}) %reduce-scatter.10.cloned.1.call-update) | async-done | bytes 2097168 | tf_op jit(solution)/shard_map/reduce_scatter | solution.py:228
  502.7 4.8 fusion.114
  515.9 7.8 multiply_reduce_fusion
  526.9 4.6 copy.211
  531.6 4.9 multiply_convert_fusion.2
  537.8 4.4 copy.208
  542.2 4.8 mul.305
  546.9 4.7 pad_maximum_fusion
  551.7 88.0 %reduce-scatter.14.cloned.1.call-done = f32[8,16,1024]{2,1,0:T(8,128)} async-done(((f32[64,16,1024]{2,1,0:T(8,128)}), f32[8,16,1024]{2,1,0:T(8,128)}) %reduce-scatter.14.cloned.1.call-update) | async-done | bytes 524304 | tf_op jit(solution)/shard_map/reduce_scatter | solution.py:281
  644.6 6.8 convolution_bitcast_fusion.2
  652.1 7.3 convolution_bitcast_fusion.3
  659.7 4.4 convolution_bitcast_fusion.5
  664.2 5.2 convolution_bitcast_fusion
  671.0 3.8 convert_reduce_fusion.2
  678.2 13.6 %all-gather.8.cloned.1.call-done = bf16[64,16,1024]{2,1,0:T(8,128)(2,1)} async-done(((bf16[8,16,1024]{2,1,0:T(8,128)(2,1)}), bf16[64,16,1024]{2,1,0:T(8,128)(2,1)}) %all-gather.8.cloned.1.call-update) | async-done | bytes 2097168 | tf_op jit(solution)/shard_map/all_gather | solution.py:282
  694.1 3.7 convolution_bitcast_fusion.1
  701.1 6.2 add_convert_fusion.1
  708.8 4.2 fusion.115
  713.0 44.5 %reduce-scatter.22.cloned.1.call-done = f32[64,512]{1,0:T(8,128)} async-done(((f32[512,512]{1,0:T(8,128)}), f32[64,512]{1,0:T(8,128)}) %reduce-scatter.22.cloned.1.call-update) | async-done | bytes 131088 | tf_op jit(solution)/shard_map/reduce_scatter | solution.py:328
  757.5 90.7 %reduce-scatter.26.cloned.1.call-done = f32[256,512]{1,0:T(8,128)} async-done(((f32[2048,512]{1,0:T(8,128)}), f32[256,512]{1,0:T(8,128)}) %reduce-scatter.26.cloned.1.call-update) | async-done | bytes 524304 | tf_op jit(solution)/shard_map/reduce_scatter | solution.py:334
  848.3 91.8 %reduce-scatter.24.cloned.1.call-done = f32[64,2048]{1,0:T(8,128)} async-done(((f32[512,2048]{1,0:T(8,128)}), f32[64,2048]{1,0:T(8,128)}) %reduce-scatter.24.cloned.1.call-update) | async-done | bytes 524304 | tf_op jit(solution)/shard_map/reduce_scatter | solution.py:332
  940.0 66.6 %reduce-scatter.18.cloned.1.call-done = f32[64,512]{1,0:T(8,128)} async-done(((f32[512,512]{1,0:T(8,128)}), f32[64,512]{1,0:T(8,128)}) %reduce-scatter.18.cloned.1.call-update) | async-done | bytes 131088 | tf_op jit(solution)/shard_map/reduce_scatter | solution.py:322
  1006.6 77.3 %reduce-scatter.20.cloned.1.call-done = f32[64,1536]{1,0:T(8,128)} async-done(((f32[512,1536]{1,0:T(8,128)}), f32[64,1536]{1,0:T(8,128)}) %reduce-scatter.20.cloned.1.call-update) | async-done | bytes 393232 | tf_op jit(solution)/shard_map/reduce_scatter | solution.py:326
  1083.9 77.4 %reduce-scatter.16.cloned.1.call-done = f32[64,1536]{1,0:T(8,128)} async-done(((f32[512,1536]{1,0:T(8,128)}), f32[64,1536]{1,0:T(8,128)}) %reduce-scatter.16.cloned.1.call-update) | async-done | bytes 393232 | tf_op jit(solution)/shard_map/reduce_scatter | solution.py:320
  1162.6 35.6 %all-reduce.12 = (f32[512]{0:T(512)S(1)}, f32[512]{0:T(512)S(1)}, f32[1024]{0:T(1024)S(1)}, f32[512]{0:T(512)S(1)}, f32[512]{0:T(512)S(1)}, /*index=5*/f32[512]{...) all-reduce(f32[512]{0:T(512)S(1)} %get-tuple-element.50, ...), channel_id=5, replica_groups=mesh['samp'=8,'feat'=4] {'samp'}, use_global_device_ids=true, to_apply=%region_26.27.clone | all-reduce | flops 8704 | bytes 69632
  1199.1 6.9 all-reduce.13
  1208.9 6.9 all-reduce.20.cloned.1.call-done
  (286 shorter events, 124.7 us)
Async XLA Ops:
  7.2 270.0 %copy-start = (bf16[512,2048]{1,0:T(8,128)(2,1)S(1)}, bf16[512,2048]{1,0:T(8,128)(2,1)}, u32[]{:S(2)}) copy-start(bf16[512,2048]{1,0:T(8,128)(2,1)} %param.39) | copy-start | bytes 6291460
  7.2 7.1 copy-start.12
  7.2 7.1 copy-start.53
  7.2 7.1 copy-start.79
  7.2 125.4 %all-reduce.18.cloned.1.call-start = ((), (), s32[]{:S(2)}) async-start(), calls=%async_computation.9 | async-start | bytes 4194304 | tf_op jit(solution)/shard_map/while/body/eval_jaxpr/psum | solution.py:15
  11.9 5.7 copy-start.37
  14.4 3.4 copy-start.42
  22.2 3.9 copy-start.21
  27.9 171.9 %all-gather.6.cloned.1.call-start = ((), (), s32[]{:S(2)}) async-start(), calls=%async_computation.11 | async-start | bytes 5242880 | tf_op jit(solution)/shard_map/all_gather | solution.py:195
  151.9 3.4 copy-start.74
  157.4 4.1 copy-start.2
  157.5 4.1 copy-start.35
  165.4 71.0 %all-gather.4.cloned.1.call-start = ((), (), s32[]{:S(2)}) async-start(), calls=%async_computation.10 | async-start | bytes 5242880 | tf_op jit(solution)/shard_map/all_gather | solution.py:196
  169.4 257.0 %reduce-scatter.12.cloned.1.call-start = ((), (), s32[]{:S(2)}) async-start(), calls=%async_computation.13 | async-start | bytes 10485760 | tf_op jit(solution)/shard_map/reduce_scatter | solution.py:229
  276.7 34.0 %copy-start.5 = (f32[64,16,512]{2,1,0:T(8,128)}, f32[64,16,512]{2,1,0:T(8,128)S(1)}, u32[]{:S(2)}) copy-start(f32[64,16,512]{2,1,0:T(8,128)S(1)} %get-tuple-element.118) | copy-start | bytes 6291460
  277.5 21.9 %copy-start.26 = (bf16[64,16,512]{2,1,0:T(8,128)(2,1)S(1)}, bf16[64,16,512]{2,1,0:T(8,128)(2,1)}, u32[]{:S(2)}) copy-start(bf16[64,16,512]{2,1,0:T(8,128)(2,1)} %param.43) | copy-start | bytes 3145732
  277.5 21.9 %copy-start.70 = (bf16[2048,512]{1,0:T(8,128)(2,1)S(1)}, bf16[2048,512]{1,0:T(8,128)(2,1)}, u32[]{:S(2)}) copy-start(bf16[2048,512]{1,0:T(8,128)(2,1)} %param.41) | copy-start | bytes 6291460
  307.3 3.3 copy-start.83
  354.5 146.2 %reduce-scatter.10.cloned.1.call-start = ((), (), s32[]{:S(2)}) async-start(), calls=%async_computation.12 | async-start | bytes 10485760 | tf_op jit(solution)/shard_map/reduce_scatter | solution.py:228
  354.5 9.1 copy-start.11
  366.2 7.4 copy-start.14
  386.5 253.2 %reduce-scatter.14.cloned.1.call-start = ((), (), s32[]{:S(2)}) async-start(), calls=%async_computation.14 | async-start | bytes 4718592 | tf_op jit(solution)/shard_map/reduce_scatter | solution.py:281
  426.4 76.2 %copy-start.36 = (f32[64,16]{1,0:T(8,128)S(1)}, f32[64,16]{1,0:T(8,128)}, u32[]{:S(2)}) copy-start(f32[64,16]{1,0:T(8,128)} %copy-done.35) | copy-start | bytes 12292
  426.4 76.2 %copy-start.59 = (f32[512]{0:T(512)S(1)}, f32[512]{0:T(512)}, u32[]{:S(2)}) copy-start(f32[512]{0:T(512)} %param.31) | copy-start | bytes 6148
  429.8 72.9 %copy-start.3 = (f32[64,16,512]{2,1,0:T(8,128)S(1)}, f32[64,16,512]{2,1,0:T(8,128)}, u32[]{:S(2)}) copy-start(f32[64,16,512]{2,1,0:T(8,128)} %copy-done.2) | copy-start | bytes 6291460
  502.6 4.8 copy-start.31
  502.6 4.8 copy-start.47
  502.6 4.8 copy-start.45
  509.2 3.7 copy-start.72
  515.9 7.8 copy-start.25
  515.9 7.8 copy-start.28
  531.6 4.9 copy-start.9
  551.7 90.0 %copy-start.23 = (bf16[64,16,512]{2,1,0:T(8,128)(2,1)S(1)}, bf16[64,16,512]{2,1,0:T(8,128)(2,1)}, u32[]{:S(2)}) copy-start(bf16[64,16,512]{2,1,0:T(8,128)(2,1)} %copy-done.22) | copy-start | bytes 3145732
  551.7 140.1 %all-gather.8.cloned.1.call-start = ((), (), s32[]{:S(2)}) async-start(), calls=%async_computation.15 | async-start | bytes 2359296 | tf_op jit(solution)/shard_map/all_gather | solution.py:282
  641.6 115.9 %reduce-scatter.22.cloned.1.call-start = ((), (), s32[]{:S(2)}) async-start(), calls=%async_computation.19 | async-start | bytes 1179648 | tf_op jit(solution)/shard_map/reduce_scatter | solution.py:328
  644.6 203.7 %reduce-scatter.26.cloned.1.call-start = ((), (), s32[]{:S(2)}) async-start(), calls=%async_computation.21 | async-start | bytes 4718592 | tf_op jit(solution)/shard_map/reduce_scatter | solution.py:334
  651.4 288.6 %reduce-scatter.24.cloned.1.call-start = ((), (), s32[]{:S(2)}) async-start(), calls=%async_computation.20 | async-start | bytes 4718592 | tf_op jit(solution)/shard_map/reduce_scatter | solution.py:332
  659.4 4.8 copy-start.30
  659.4 4.7 copy-start.78
  659.4 347.2 %reduce-scatter.18.cloned.1.call-start = ((), (), s32[]{:S(2)}) async-start(), calls=%async_computation.17 | async-start | bytes 1179648 | tf_op jit(solution)/shard_map/reduce_scatter | solution.py:322
  664.1 419.8 %reduce-scatter.20.cloned.1.call-start = ((), (), s32[]{:S(2)}) async-start(), calls=%async_computation.18 | async-start | bytes 3538944 | tf_op jit(solution)/shard_map/reduce_scatter | solution.py:326
  669.4 491.9 %reduce-scatter.16.cloned.1.call-start = ((), (), s32[]{:S(2)}) async-start(), calls=%async_computation.16 | async-start | bytes 3538944 | tf_op jit(solution)/shard_map/reduce_scatter | solution.py:320
  697.9 518.0 %all-reduce.20.cloned.1.call-start = ((), (), s32[]{:S(2)}) async-start(), calls=%async_computation.22 | async-start | bytes 4194304 | tf_op jit(solution)/shard_map/psum | solution.py:294
  701.1 6.3 copy-start.57
  708.8 4.2 copy-start.49
  1215.8 6.8 copy-start.40
  1215.8 7.6 copy-start.39
  1215.8 8.4 copy-start.1
  (50 other events, 89.2 us)
Sparse Core Ops, SparseCore 0:
  28.0 104.5 all-reduce.17
  165.5 34.1 all-gather.5
  201.9 34.4 all-gather.3
  354.6 71.7 reduce-scatter.11
  429.0 71.6 reduce-scatter.9
  551.8 87.9 reduce-scatter.13
  642.7 49.0 all-gather.7
  695.6 61.9 reduce-scatter.21
  761.1 87.0 reduce-scatter.25
  852.2 87.8 reduce-scatter.23
  943.5 63.0 reduce-scatter.17
  1010.5 73.4 reduce-scatter.19
  1087.9 73.3 reduce-scatter.15
  1164.1 51.6 all-reduce.19
where the time goes:
time: 1240 us; the launch traced here: 1230 us
  waiting for transfers between devices  795 us (64%)
  matrix products  188 us (15%)
  local copies, waits for them, and re-layouts  132 us (11%)
  other arithmetic  52.2 us (4%)
  blocking collectives  42.5 us (3%)
  between operations  19.7 us (2%)
    psum x1, waiting for transfers between devices, spread_2(): return lax.psum(block, axis)  98.7 us
    reduce_scatter x1, waiting for transfers between devices, local(): lax.psum_scatter(summed[14], 'samp', scatter_dimension=0, tiled=True)  91.8 us
    reduce_scatter x1, waiting for transfers between devices, local(): lax.psum_scatter(summed[16], 'samp', scatter_dimension=0, tiled=True)  90.7 us
    reduce_scatter x1, waiting for transfers between devices, local(): lax.psum_scatter(term_block, 'samp', scatter_dimension=0, tiled=True)  88 us
    reduce_scatter x1, waiting for transfers between devices, local(): lax.psum_scatter(summed[2], 'samp', scatter_dimension=0, tiled=True)  77.4 us
    reduce_scatter x1, waiting for transfers between devices, local(): lax.psum_scatter(summed[8], 'samp', scatter_dimension=0, tiled=True)  77.3 us
    reduce_scatter x1, waiting for transfers between devices, local(): lax.psum_scatter(grad_keys, 'feat', scatter_dimension=1, tiled=True)  71 us
    reduce_scatter x1, waiting for transfers between devices, local(): lax.psum_scatter(summed[4], 'samp', scatter_dimension=0, tiled=True)  66.6 us
  transfers between devices with their start and end apart: 14, of which 14 were waited for; matrix products, arithmetic and copies ran while one was open for 11% of the time, Pallas kernels for 0%

commit v1 on v0

--- a/solution.py
+++ b/solution.py
@@ -12,7 +12,7 @@
 
 def spread_2(block, axis, owner):
     block = jnp.where(lax.axis_index(axis) == owner, block, jnp.zeros_like(block))
-    return lax.psum(block, axis)
+    return jnp.sum(lax.all_gather(block, axis), axis=0)
 
 
 def layer_norm(values, gain_row, shift_row):

time: 1240 us -> 1370 us (1.10)
  waiting for transfers between devices: 795 us -> 920 us
    all_gather x0 -> x1, waiting for transfers between devices: none -> 224 us  [spread_2(): return jnp.sum(lax.all_gather(block, axis), axis=0)]
    psum x1 -> x0, waiting for transfers between devices: 98.7 us -> none  [spread_2(): return lax.psum(block, axis)]
    reshape x8 -> x7, local copies, waits for them, and re-layouts: 40.7 us -> 37.1 us  [split_heads(): return values.reshape(values.shape[0], values.shape[1], HEADS, HEAD_DIM)]
  transfers between devices with their start and end apart: 14 -> 14, of which waited for: 14 -> 14; matrix products, arithmetic and copies ran while one was open for 11% -> 10% of each run, Pallas kernels for 0% -> 0%
where the time goes in v1:
time: 1370 us; the launch traced here: 1360 us
  waiting for transfers between devices  920 us (67%)
  matrix products  186 us (14%)
  local copies, waits for them, and re-layouts  131 us (10%)
  other arithmetic  63.1 us (5%)
  blocking collectives  42.5 us (3%)
  between operations  19.9 us (1%)
    all_gather x1, waiting for transfers between devices, spread_2(): return jnp.sum(lax.all_gather(block, axis), axis=0)  224 us
    reduce_scatter x1, waiting for transfers between devices, local(): lax.psum_scatter(summed[14], 'samp', scatter_dimension=0, tiled=True)  91.6 us
    reduce_scatter x1, waiting for transfers between devices, local(): lax.psum_scatter(summed[16], 'samp', scatter_dimension=0, tiled=True)  90.8 us
    reduce_scatter x1, waiting for transfers between devices, local(): lax.psum_scatter(term_block, 'samp', scatter_dimension=0, tiled=True)  88.2 us
    reduce_scatter x1, waiting for transfers between devices, local(): lax.psum_scatter(summed[8], 'samp', scatter_dimension=0, tiled=True)  77.4 us
    reduce_scatter x1, waiting for transfers between devices, local(): lax.psum_scatter(summed[2], 'samp', scatter_dimension=0, tiled=True)  77.4 us
    reduce_scatter x1, waiting for transfers between devices, local(): lax.psum_scatter(grad_keys, 'feat', scatter_dimension=1, tiled=True)  71 us
    reduce_scatter x1, waiting for transfers between devices, local(): lax.psum_scatter(summed[4], 'samp', scatter_dimension=0, tiled=True)  66.6 us
  transfers between devices with their start and end apart: 14, of which 14 were waited for; matrix products, arithmetic and copies ran while one was open for 10% of the time, Pallas kernels for 0%

profile of v1, /device:TPU:0, one launch (start us, length us, event | category | flops | bytes accessed | tf_op | source)
XLA Modules:
  0.0 1364.1 jit_solution(15496879198896697891)
XLA Ops:
  22.1 3.9 fusion.41
  33.9 224.5 %all-gather.5.cloned.1.call-done = bf16[8,64,16,1024]{3,2,1,0:T(8,128)(2,1)} async-done(((bf16[1,64,16,1024]{3,2,1,0:T(8,128)(2,1)}), bf16[8,64,16,1024]{3,2,1,0:T(8,128)(2,1)}) %all-gather.5.cloned.1.call-update) | async-done | bytes 16777232 | tf_op jit(solution)/shard_map/while/body/eval_jaxpr/all_gather | solution.py:15
  258.4 10.8 reduce_sum.303
  272.3 3.9 reshape.325
  279.3 4.0 fusion.65
  301.0 3.9 fusion.40
  307.2 26.5 %all-gather.9.cloned.1.call-done = bf16[64,64,512]{2,1,0:T(8,128)(2,1)} async-done(((bf16[64,16,512]{2,1,0:T(8,128)(2,1)}), bf16[64,64,512]{2,1,0:T(8,128)(2,1)}) %all-gather.9.cloned.1.call-update) | async-done | bytes 4194320 | tf_op jit(solution)/shard_map/all_gather | solution.py:195
  333.7 11.4 reshape.328
  345.1 8.5 fusion.21
  358.8 11.6 all-gather.7.cloned.1.call-done
  370.4 11.2 reshape.326
  381.5 19.2 %convert_bitcast_fusion = bf16[64,16,8,64]{3,1,2,0:T(8,128)(2,1)} fusion(bf16[64,64,8,64]{3,2,1,0:T(8,128)(2,1)} %reshape.326, f32[64,8,16]{2,1,0:T(8,128)S(1)} %get-tuple-element.115, f32[64,8,16,64]{3,2,1,0:T(8,128)} %copy-done.10), kind=kOutput, calls=%fused_computation.111 | convolution fusion | flops 70262848 | bytes 7372800 | tf_op jit(solution)/shard_map/shfg,sghd->sfhd/dot_general | solution.py:76
  411.2 21.9 %multiply_convert_fusion = (bf16[64,16,2048]{2,1,0:T(8,128)(2,1)}, f32[64,16,2048]{2,1,0:T(8,128)S(1)}, f32[64,16,2048]{2,1,0:T(8,128)}) fusion(f32[2048]{0:T(1024)S(1)} %copy-done.73, bf16[512,2048]{1,0:T(8,128)(2,1)S(1)} %copy-done, f32[64,16,512]{2,1,0:T(8,128)S(1)} %get-tuple-element.118, f32[512]{0:T(512)S(1)} %copy-done.75, f32[512]{0:T(512)S(1)} %copy-done.65, ...), kind=kOutput, calls=%fused_computation.15 | convolution fusion | flops 2288517120 | bytes 25186304 | tf_op jit(solution)/shard_map/sfd,de->sfe/dot_general | solution.py:26
  433.1 7.9 convert_reduce_fusion
  452.4 23.3 %fusion.59 = f32[64,8,64,64]{3,2,1,0:T(8,128)} fusion(bf16[64,16,8,64]{3,2,1,0:T(8,128)(2,1)S(1)} %reshape.329, f32[64,8,16]{2,1,0:T(8,128)S(1)} %get-tuple-element.115, f32[64,8,16,64]{3,2,1,0:T(8,128)} %copy-done.10), kind=kOutput, calls=%fused_computation.123 | convolution fusion | flops 69738560 | bytes 11567104 | tf_op jit(solution)/shard_map/shfg,sfhd->sghd/dot_general | solution.py:108
  475.7 12.7 copy.164
  488.5 9.1 multiply_reduce_fusion.1
  500.2 7.4 convolution_multiply_fusion
  507.6 12.9 copy.162
  522.3 6.3 convert_reduce_fusion.1
  531.3 29.0 %reduce-scatter.12.cloned.1.call-done = f32[64,16,512]{2,1,0:T(8,128)} async-done(((f32[64,64,512]{2,1,0:T(8,128)}), f32[64,16,512]{2,1,0:T(8,128)}) %reduce-scatter.12.cloned.1.call-update) | async-done | bytes 2097168 | tf_op jit(solution)/shard_map/reduce_scatter | solution.py:229
  563.7 71.0 %reduce-scatter.10.cloned.1.call-done = f32[64,16,512]{2,1,0:T(8,128)} async-done(((f32[64,64,512]{2,1,0:T(8,128)}), f32[64,16,512]{2,1,0:T(8,128)}) %reduce-scatter.10.cloned.1.call-update) | async-done | bytes 2097168 | tf_op jit(solution)/shard_map/reduce_scatter | solution.py:228
  636.6 4.8 fusion.113
  649.9 6.6 multiply_reduce_fusion
  659.7 4.3 copy.176
  664.0 4.9 multiply_convert_fusion.2
  670.2 4.4 copy.173
  674.6 5.0 mul.305
  679.6 4.7 pad_maximum_fusion
  684.4 88.2 %reduce-scatter.14.cloned.1.call-done = f32[8,16,1024]{2,1,0:T(8,128)} async-done(((f32[64,16,1024]{2,1,0:T(8,128)}), f32[8,16,1024]{2,1,0:T(8,128)}) %reduce-scatter.14.cloned.1.call-update) | async-done | bytes 524304 | tf_op jit(solution)/shard_map/reduce_scatter | solution.py:281
  777.4 6.8 convolution_bitcast_fusion.2
  784.9 7.3 convolution_bitcast_fusion.3
  792.2 4.4 convolution_bitcast_fusion.5
  796.8 5.2 convolution_bitcast_fusion
  803.6 3.8 convert_reduce_fusion.2
  810.8 13.7 %all-gather.11.cloned.1.call-done = bf16[64,16,1024]{2,1,0:T(8,128)(2,1)} async-done(((bf16[8,16,1024]{2,1,0:T(8,128)(2,1)}), bf16[64,16,1024]{2,1,0:T(8,128)(2,1)}) %all-gather.11.cloned.1.call-update) | async-done | bytes 2097168 | tf_op jit(solution)/shard_map/all_gather | solution.py:282
  826.9 3.7 convolution_bitcast_fusion.1
  833.9 6.2 add_convert_fusion.1
  841.6 4.2 fusion.114
  845.8 44.5 %reduce-scatter.22.cloned.1.call-done = f32[64,512]{1,0:T(8,128)} async-done(((f32[512,512]{1,0:T(8,128)}), f32[64,512]{1,0:T(8,128)}) %reduce-scatter.22.cloned.1.call-update) | async-done | bytes 131088 | tf_op jit(solution)/shard_map/reduce_scatter | solution.py:328
  890.3 90.8 %reduce-scatter.26.cloned.1.call-done = f32[256,512]{1,0:T(8,128)} async-done(((f32[2048,512]{1,0:T(8,128)}), f32[256,512]{1,0:T(8,128)}) %reduce-scatter.26.cloned.1.call-update) | async-done | bytes 524304 | tf_op jit(solution)/shard_map/reduce_scatter | solution.py:334
  981.1 91.6 %reduce-scatter.24.cloned.1.call-done = f32[64,2048]{1,0:T(8,128)} async-done(((f32[512,2048]{1,0:T(8,128)}), f32[64,2048]{1,0:T(8,128)}) %reduce-scatter.24.cloned.1.call-update) | async-done | bytes 524304 | tf_op jit(solution)/shard_map/reduce_scatter | solution.py:332
  1072.7 66.6 %reduce-scatter.18.cloned.1.call-done = f32[64,512]{1,0:T(8,128)} async-done(((f32[512,512]{1,0:T(8,128)}), f32[64,512]{1,0:T(8,128)}) %reduce-scatter.18.cloned.1.call-update) | async-done | bytes 131088 | tf_op jit(solution)/shard_map/reduce_scatter | solution.py:322
  1139.3 77.4 %reduce-scatter.20.cloned.1.call-done = f32[64,1536]{1,0:T(8,128)} async-done(((f32[512,1536]{1,0:T(8,128)}), f32[64,1536]{1,0:T(8,128)}) %reduce-scatter.20.cloned.1.call-update) | async-done | bytes 393232 | tf_op jit(solution)/shard_map/reduce_scatter | solution.py:326
  1216.8 77.4 %reduce-scatter.16.cloned.1.call-done = f32[64,1536]{1,0:T(8,128)} async-done(((f32[512,1536]{1,0:T(8,128)}), f32[64,1536]{1,0:T(8,128)}) %reduce-scatter.16.cloned.1.call-update) | async-done | bytes 393232 | tf_op jit(solution)/shard_map/reduce_scatter | solution.py:320
  1295.5 35.6 %all-reduce.12 = (f32[512]{0:T(512)S(1)}, f32[512]{0:T(512)S(1)}, f32[1024]{0:T(1024)S(1)}, f32[512]{0:T(512)S(1)}, f32[512]{0:T(512)S(1)}, /*index=5*/f32[512]{...) all-reduce(f32[512]{0:T(512)S(1)} %get-tuple-element.50, ...), channel_id=5, replica_groups=mesh['samp'=8,'feat'=4] {'samp'}, use_global_device_ids=true, to_apply=%region_26.27.clone | all-reduce | flops 8704 | bytes 69632
  1332.0 6.9 all-reduce.13
  1341.7 6.9 all-reduce.17.cloned.1.call-done
  (287 shorter events, 127.5 us)
Async XLA Ops:
  7.2 403.7 %copy-start = (bf16[512,2048]{1,0:T(8,128)(2,1)S(1)}, bf16[512,2048]{1,0:T(8,128)(2,1)}, u32[]{:S(2)}) copy-start(bf16[512,2048]{1,0:T(8,128)(2,1)} %param.39) | copy-start | bytes 6291460
  7.2 7.1 copy-start.12
  7.2 7.1 copy-start.53
  7.2 7.1 copy-start.79
  7.2 251.2 %all-gather.5.cloned.1.call-start = ((), (), s32[]{:S(2)}) async-start(), calls=%async_computation.9 | async-start | bytes 18874368 | tf_op jit(solution)/shard_map/while/body/eval_jaxpr/all_gather | solution.py:15
  11.9 5.7 copy-start.37
  14.4 3.3 copy-start.42
  22.1 3.9 copy-start.21
  27.9 305.8 %all-gather.9.cloned.1.call-start = ((), (), s32[]{:S(2)}) async-start(), calls=%async_computation.11 | async-start | bytes 5242880 | tf_op jit(solution)/shard_map/all_gather | solution.py:195
  287.3 3.4 copy-start.74
  292.9 4.1 copy-start.2
  293.0 4.1 copy-start.35
  300.9 69.5 %all-gather.7.cloned.1.call-start = ((), (), s32[]{:S(2)}) async-start(), calls=%async_computation.10 | async-start | bytes 5242880 | tf_op jit(solution)/shard_map/all_gather | solution.py:196
  304.8 255.5 %reduce-scatter.12.cloned.1.call-start = ((), (), s32[]{:S(2)}) async-start(), calls=%async_computation.13 | async-start | bytes 10485760 | tf_op jit(solution)/shard_map/reduce_scatter | solution.py:229
  410.4 34.0 %copy-start.5 = (f32[64,16,512]{2,1,0:T(8,128)}, f32[64,16,512]{2,1,0:T(8,128)S(1)}, u32[]{:S(2)}) copy-start(f32[64,16,512]{2,1,0:T(8,128)S(1)} %get-tuple-element.118) | copy-start | bytes 6291460
  411.2 21.9 %copy-start.26 = (bf16[64,16,512]{2,1,0:T(8,128)(2,1)S(1)}, bf16[64,16,512]{2,1,0:T(8,128)(2,1)}, u32[]{:S(2)}) copy-start(bf16[64,16,512]{2,1,0:T(8,128)(2,1)} %param.43) | copy-start | bytes 3145732
  411.2 21.9 %copy-start.70 = (bf16[2048,512]{1,0:T(8,128)(2,1)S(1)}, bf16[2048,512]{1,0:T(8,128)(2,1)}, u32[]{:S(2)}) copy-start(bf16[2048,512]{1,0:T(8,128)(2,1)} %param.41) | copy-start | bytes 6291460
  441.1 3.3 copy-start.83
  488.4 146.2 %reduce-scatter.10.cloned.1.call-start = ((), (), s32[]{:S(2)}) async-start(), calls=%async_computation.12 | async-start | bytes 10485760 | tf_op jit(solution)/shard_map/reduce_scatter | solution.py:228
  488.5 9.1 copy-start.11
  500.1 7.5 copy-start.14
  520.5 252.0 %reduce-scatter.14.cloned.1.call-start = ((), (), s32[]{:S(2)}) async-start(), calls=%async_computation.14 | async-start | bytes 4718592 | tf_op jit(solution)/shard_map/reduce_scatter | solution.py:281
  560.3 76.2 %copy-start.36 = (f32[64,16]{1,0:T(8,128)S(1)}, f32[64,16]{1,0:T(8,128)}, u32[]{:S(2)}) copy-start(f32[64,16]{1,0:T(8,128)} %copy-done.35) | copy-start | bytes 12292
  560.3 76.2 %copy-start.59 = (f32[512]{0:T(512)S(1)}, f32[512]{0:T(512)}, u32[]{:S(2)}) copy-start(f32[512]{0:T(512)} %param.31) | copy-start | bytes 6148
  563.7 72.9 %copy-start.3 = (f32[64,16,512]{2,1,0:T(8,128)S(1)}, f32[64,16,512]{2,1,0:T(8,128)}, u32[]{:S(2)}) copy-start(f32[64,16,512]{2,1,0:T(8,128)} %copy-done.2) | copy-start | bytes 6291460
  636.5 4.8 copy-start.31
  636.6 4.8 copy-start.47
  636.6 4.8 copy-start.45
  643.2 3.7 copy-start.72
  649.9 6.7 copy-start.25
  649.9 6.7 copy-start.28
  664.0 4.9 copy-start.9
  684.3 90.1 %copy-start.23 = (bf16[64,16,512]{2,1,0:T(8,128)(2,1)S(1)}, bf16[64,16,512]{2,1,0:T(8,128)(2,1)}, u32[]{:S(2)}) copy-start(bf16[64,16,512]{2,1,0:T(8,128)(2,1)} %copy-done.22) | copy-start | bytes 3145732
  684.3 140.2 %all-gather.11.cloned.1.call-start = ((), (), s32[]{:S(2)}) async-start(), calls=%async_computation.15 | async-start | bytes 2359296 | tf_op jit(solution)/shard_map/all_gather | solution.py:282
  774.3 116.0 %reduce-scatter.22.cloned.1.call-start = ((), (), s32[]{:S(2)}) async-start(), calls=%async_computation.19 | async-start | bytes 1179648 | tf_op jit(solution)/shard_map/reduce_scatter | solution.py:328
  777.3 203.8 %reduce-scatter.26.cloned.1.call-start = ((), (), s32[]{:S(2)}) async-start(), calls=%async_computation.21 | async-start | bytes 4718592 | tf_op jit(solution)/shard_map/reduce_scatter | solution.py:334
  784.2 288.5 %reduce-scatter.24.cloned.1.call-start = ((), (), s32[]{:S(2)}) async-start(), calls=%async_computation.20 | async-start | bytes 4718592 | tf_op jit(solution)/shard_map/reduce_scatter | solution.py:332
  792.2 4.6 copy-start.30
  792.2 4.6 copy-start.78
  792.2 347.1 %reduce-scatter.18.cloned.1.call-start = ((), (), s32[]{:S(2)}) async-start(), calls=%async_computation.17 | async-start | bytes 1179648 | tf_op jit(solution)/shard_map/reduce_scatter | solution.py:322
  796.7 420.1 %reduce-scatter.20.cloned.1.call-start = ((), (), s32[]{:S(2)}) async-start(), calls=%async_computation.18 | async-start | bytes 3538944 | tf_op jit(solution)/shard_map/reduce_scatter | solution.py:326
  802.0 492.2 %reduce-scatter.16.cloned.1.call-start = ((), (), s32[]{:S(2)}) async-start(), calls=%async_computation.16 | async-start | bytes 3538944 | tf_op jit(solution)/shard_map/reduce_scatter | solution.py:320
  830.6 518.1 %all-reduce.17.cloned.1.call-start = ((), (), s32[]{:S(2)}) async-start(), calls=%async_computation.22 | async-start | bytes 4194304 | tf_op jit(solution)/shard_map/psum | solution.py:294
  833.9 6.3 copy-start.57
  841.6 4.2 copy-start.49
  1348.7 6.8 copy-start.40
  1348.7 7.6 copy-start.39
  1348.7 8.4 copy-start.1
  (50 other events, 88.4 us)
Sparse Core Ops, SparseCore 0:
  28.1 230.3 all-gather.4
  301.0 32.6 all-gather.8
  335.9 34.4 all-gather.6
  488.6 71.7 reduce-scatter.11
  562.9 71.6 reduce-scatter.9
  684.4 88.0 reduce-scatter.13
  775.4 49.0 all-gather.10
  828.3 61.9 reduce-scatter.21
  894.0 87.0 reduce-scatter.25
  985.0 87.6 reduce-scatter.23
  1076.1 63.1 reduce-scatter.17
  1143.2 73.5 reduce-scatter.19
  1220.8 73.3 reduce-scatter.15
  1297.0 51.6 all-reduce.16
